TPU v7x, 32 devices: a whole 2x2x4 slice. The times are simulated.
32 devices in a mesh: groups: 2 (over y), blk: 4 (over z), tok: 4 (over x, core).
Axes of the slice: x: 2, y: 2, z: 4, core: 2. Of those that a mesh axis runs over, the one named last changes fastest.
Arguments:
- inputs: bfloat16 [12288, 2048], P(('groups', 'tok'), 'blk'), parts along dimension 0, may hold values from -6 to 6
- targets: bfloat16 [12288, 2048], P(('groups', 'tok'), 'blk'), parts along dimension 0, may hold values from -6 to 6
- left_factor: bfloat16 [16, 256, 256], P(('groups', 'blk')), parts along dimension 0, may hold values from -0.375 to 0.375
- right_factor: bfloat16 [16, 256, 256], P(('groups', 'blk')), parts along dimension 0, may hold values from -0.375 to 0.375
Outputs:
- grad_left: float32 [16, 256, 256], P(('groups', 'blk'), 'tok'), parts along dimension 0
- grad_right: float32 [16, 256, 256], P(('groups', 'blk'), 'tok'), parts along dimension 0
There are 2 independent parts, one for each index of `groups`. A program takes and returns all parts, laid end to end along the dimension named above; each array names one. Nothing has to cross between parts.
All inputs are finite; a program needn't handle non-finite values.
Results may differ from a plain program's by a relative error of at most 0.0015.
Values may be sent and summed in bfloat16 or wider, within the bound.
No kernel may reach another device: no remote copies, remote signals or barrier semaphores. Data moves between devices by JAX's collectives and lax.ppermute only.
A program may use at most 64 MiB of HBM per device.

v0:
```python
import jax
import jax.numpy as jnp
from jax import lax
from jax.sharding import PartitionSpec as P


def on_device(inputs, targets, left_factor, right_factor):
    local_blocks = left_factor.shape[0]
    block_width = left_factor.shape[1]
    tok_rows = inputs.shape[0]
    peer_count = lax.axis_size("blk")
    all_blocks = local_blocks * peer_count
    stride_len = block_width // all_blocks
    shaped = inputs.reshape(tok_rows, local_blocks, block_width)
    first_out = jnp.einsum(
        "tki,kji->kjt", shaped, left_factor, preferred_element_type=jnp.float32
    ).astype(jnp.bfloat16)
    outgoing = first_out.reshape(local_blocks, peer_count, local_blocks, stride_len, tok_rows)
    right_view = right_factor.reshape(local_blocks, block_width, all_blocks, stride_len)
    arrived = lax.all_to_all(outgoing, "blk", split_axis=1, concat_axis=0, tiled=True)
    mixed_part = arrived[:, 0]
    student_part = jnp.einsum(
        "gokm,kgmt->got", right_view, mixed_part, preferred_element_type=jnp.float32
    )
    student_four = student_part[:, :, None, :]
    student = student_four[:, :, 0, :]
    truth = targets.reshape(tok_rows, local_blocks, block_width).transpose(1, 2, 0)
    error_rows = (student - truth.astype(jnp.float32)).astype(jnp.bfloat16)
    inverse_rows = jnp.float32(1.0 / tok_rows)
    term_right = jnp.einsum(
        "got,kgmt->gokm", error_rows, mixed_part, preferred_element_type=jnp.float32
    ).reshape(local_blocks, block_width, block_width)
    backward_in = jnp.einsum(
        "gokm,got->kgmt", right_view, error_rows, preferred_element_type=jnp.float32
    ).astype(jnp.bfloat16)
    returned = lax.all_to_all(backward_in, "blk", split_axis=0, concat_axis=1, tiled=True)
    back_first = returned.reshape(local_blocks, block_width, tok_rows)
    term_left = jnp.einsum("kjt,tki->kji", back_first, shaped, preferred_element_type=jnp.float32)
    summed_left, summed_right = (
        lax.psum_scatter(term_left, "tok", scatter_dimension=1, tiled=True),
        lax.psum_scatter(term_right, "tok", scatter_dimension=1, tiled=True),
    )
    return (summed_left * inverse_rows, summed_right * inverse_rows)


def solution(mesh):
    in_specs = (
        P(("groups", "tok"), "blk"),
        P(("groups", "tok"), "blk"),
        P(("groups", "blk"), None, None),
        P(("groups", "blk"), None, None),
    )
    out_specs = (P(("groups", "blk"), "tok", None), P(("groups", "blk"), "tok", None))
    return jax.shard_map(
        on_device, mesh=mesh, in_specs=in_specs, out_specs=out_specs, check_vma=False
    )
```

profile of v0, /device:TPU:0, one launch (start us, length us, event | category | flops | bytes accessed | tf_op | source)
XLA Modules:
  0.0 133.3 jit_solution(9672742158649602140)
XLA Ops:
  7.2 0.9 copy-done
  8.1 2.0 %convolution_convert_fusion = bf16[2,256,1536]{2,1,0:T(8,128)(2,1)S(1)} fusion(bf16[2,256,256]{2,1,0:T(8,128)(2,1)S(1)} %copy-done, bf16[192,2,8,256]{3,2,1,0:T(8,128)(2,1)} %bitcast.57), kind=kOutput, calls=%fused_computation.3 | convolution fusion | flops 403439616 | bytes 3407872 | tf_op jit(solution)/shard_map/tki,kji->kjt/dot_general | solution.py:15
  10.1 1.3 copy.26
  11.4 6.5 %all-to-all-start = ((bf16[2,4,2,32,1536]{4,3,2,0,1:T(8,128)(2,1)}), bf16[2,4,2,32,1536]{4,3,2,0,1:T(8,128)(2,1)S(1)}, u32[]{:S(2)}, u32[]{:S(2)}) async-start(bf16[2,4,2,32,1536]{4,3,2,0,1:T(8,128)(2,1)} %copy.26), calls=%async_computation | async-start | bytes 3145728 | tf_op jit(solution)/shard_map/all_to_all | solution.py:20
  17.9 0.8 copy.28
  18.7 1.7 %copy.29 = bf16[1536,512]{0,1:T(8,128)(2,1)S(1)} copy(bf16[1536,512]{1,0:T(8,128)(2,1)} %param.5) | data formatting | bytes 3145728 | tf_op args[1]
  20.4 2.0 %copy.30 = f32[1536,2,256]{2,0,1:T(8,128)} copy(bf16[1536,2,256]{0,2,1:T(8,128)(2,1)S(1)} %bitcast.53) | data formatting | bytes 4718592 | tf_op jit(solution)/shard_map/convert_element_type | solution.py:28
  22.5 32.4 %all-to-all-done = bf16[2,4,2,32,1536]{4,3,2,0,1:T(8,128)(2,1)S(1)} async-done(((bf16[2,4,2,32,1536]{4,3,2,0,1:T(8,128)(2,1)}), bf16[2,4,2,32,1536]{4,3,2,0,1:T(8,128)(2,1)S(1)}, u32[]{:S(2)}, u32[]{:S(2)}) %all-to-all-start) | async-done | bytes 1572896 | tf_op jit(solution)/shard_map/all_to_all | solution.py:20
  54.8 0.1 copy.27
  55.0 2.3 %copy-done.1 = f32[1536,2,256]{2,0,1:T(8,128)S(1)} copy-done((f32[1536,2,256]{2,0,1:T(8,128)S(1)}, f32[1536,2,256]{2,0,1:T(8,128)}, u32[]{:S(2)}) %copy-start.1) | copy-done | bytes 3145752
  57.3 1.8 %fusion.1 = bf16[2,256,1536]{1,2,0:T(8,128)(2,1)S(1)} fusion(f32[1536,2,256]{2,0,1:T(8,128)S(1)} %copy-done.1, bf16[8,2,32,1536]{3,2,0,1:T(8,128)(2,1)S(1)} %bitcast.54, bf16[2,256,8,32]{1,3,2,0:T(8,128)(2,1)} %bitcast.60), kind=kOutput, calls=%fused_computation.2 | convolution fusion | flops 404226048 | bytes 6553600 | tf_op jit(solution)/shard_map/gokm,kgmt->got/dot_general | solution.py:22
  59.1 0.6 fusion.9
  59.7 0.2 convert_bitcast_fusion
  59.9 1.3 copy.32
  61.2 3.6 %all-to-all-start.1 = ((bf16[8,2,32,1536]{3,2,1,0:T(8,128)(2,1)}), bf16[8,2,32,1536]{3,2,1,0:T(8,128)(2,1)S(1)}, u32[]{:S(2)}, u32[]{:S(2)}) async-start(bf16[8,2,32,1536]{3,2,1,0:T(8,128)(2,1)} %copy.32), calls=%async_computation.1 | async-start | bytes 3145728 | tf_op jit(solution)/shard_map/all_to_all | solution.py:36
  64.8 2.8 %fusion.5 = f32[2,256,8,32]{1,3,2,0:T(8,128)} fusion(bf16[8,2,32,1536]{3,2,0,1:T(8,128)(2,1)} %bitcast.55, bf16[2,256,1536]{1,2,0:T(8,128)(2,1)S(1)} %fusion.1), kind=kOutput, calls=%fused_computation.7 | convolution fusion | flops 402653184 | bytes 3670016 | tf_op jit(solution)/shard_map/got,kgmt->gokm/dot_general | solution.py:30
  67.6 2.0 %copy.36 = f32[2,256,256]{2,1,0:T(8,128)} copy(f32[2,256,256]{1,2,0:T(8,128)} %bitcast.59) | data formatting | bytes 1048576 | tf_op jit(solution)/shard_map/reshape | solution.py:32
  69.7 31.5 %all-to-all-done.1 = bf16[8,2,32,1536]{3,2,1,0:T(8,128)(2,1)S(1)} async-done(((bf16[8,2,32,1536]{3,2,1,0:T(8,128)(2,1)}), bf16[8,2,32,1536]{3,2,1,0:T(8,128)(2,1)S(1)}, u32[]{:S(2)}, u32[]{:S(2)}) %all-to-all-start.1) | async-done | bytes 1572896 | tf_op jit(solution)/shard_map/all_to_all | solution.py:36
  101.2 0.1 copy.33
  101.3 1.3 copy-done.3
  102.6 1.4 %fusion.2 = f32[2,256,256]{2,1,0:T(8,128)} fusion(bf16[2,256,1536]{2,1,0:T(8,128)(2,1)S(1)} %bitcast.56, bf16[192,2,8,256]{3,2,1,0:T(8,128)(2,1)S(1)} %bitcast.58), kind=kOutput, calls=%fused_computation.4 | convolution fusion | flops 402653184 | bytes 3670016 | tf_op jit(solution)/shard_map/kjt,tki->kji/dot_general | solution.py:38
  104.0 1.6 %broadcast_multiply_fusion = f32[2,64,256]{2,1,0:T(8,128)} fusion(f32[2,64,256]{2,1,0:T(8,128)} %reduce-scatter.5.cloned.1.call-done), kind=kLoop, calls=%fused_computation.12 | loop fusion | flops 32768 | bytes 262144 | tf_op jit(solution)/shard_map/mul | solution.py:43
  105.6 19.3 %reduce-scatter.3.cloned.1.call-done = f32[2,64,256]{2,1,0:T(8,128)} async-done(((f32[2,256,256]{2,1,0:T(8,128)}), f32[2,64,256]{2,1,0:T(8,128)}) %reduce-scatter.3.cloned.1.call-update) | async-done | bytes 131088 | tf_op jit(solution)/shard_map/reduce_scatter | solution.py:40
  124.9 1.6 %broadcast_multiply_fusion.1 = f32[2,64,256]{2,1,0:T(8,128)} fusion(f32[2,64,256]{2,1,0:T(8,128)} %reduce-scatter.3.cloned.1.call-done), kind=kLoop, calls=%fused_computation.13 | loop fusion | flops 32768 | bytes 262144 | tf_op jit(solution)/shard_map/mul | solution.py:43
  (14 shorter events, 0.2 us)
Async XLA Ops:
  7.2 1.0 copy-start
  11.4 6.5 %copy-start.4 = (bf16[2,256,256]{2,1,0:T(8,128)(2,1)S(1)}, bf16[2,256,256]{2,1,0:T(8,128)(2,1)}, u32[]{:S(2)}) copy-start(bf16[2,256,256]{2,1,0:T(8,128)(2,1)} %param.7) | copy-start | bytes 786436
  11.4 43.4 %all-to-all-start = ((bf16[2,4,2,32,1536]{4,3,2,0,1:T(8,128)(2,1)}), bf16[2,4,2,32,1536]{4,3,2,0,1:T(8,128)(2,1)S(1)}, u32[]{:S(2)}, u32[]{:S(2)}) async-start(bf16[2,4,2,32,1536]{4,3,2,0,1:T(8,128)(2,1)} %copy.26), calls=%async_computation | async-start | bytes 3145728 | tf_op jit(solution)/shard_map/all_to_all | solution.py:20
  54.8 2.5 %copy-start.1 = (f32[1536,2,256]{2,0,1:T(8,128)S(1)}, f32[1536,2,256]{2,0,1:T(8,128)}, u32[]{:S(2)}) copy-start(f32[1536,2,256]{2,0,1:T(8,128)} %copy.30) | copy-start | bytes 9437188
  54.9 4.1 %copy-start.2 = (bf16[4,2,1,2,32,1536]{5,4,1,0,3,2:T(8,128)(2,1)}, bf16[4,2,1,2,32,1536]{5,4,1,0,3,2:T(8,128)(2,1)S(1)}, u32[]{:S(2)}) copy-start(bf16[4,2,1,2,32,1536]{5,4,1,0,3,2:T(8,128)(2,1)S(1)} %copy.27) | copy-start | bytes 4718596
  57.3 1.8 %copy-start.5 = (bf16[2,256,256]{2,1,0:T(8,128)(2,1)S(1)}, bf16[2,256,256]{2,1,0:T(8,128)(2,1)}, u32[]{:S(2)}) copy-start(bf16[2,256,256]{2,1,0:T(8,128)(2,1)} %param.7) | copy-start | bytes 786436
  61.2 40.0 %all-to-all-start.1 = ((bf16[8,2,32,1536]{3,2,1,0:T(8,128)(2,1)}), bf16[8,2,32,1536]{3,2,1,0:T(8,128)(2,1)S(1)}, u32[]{:S(2)}, u32[]{:S(2)}) async-start(bf16[8,2,32,1536]{3,2,1,0:T(8,128)(2,1)} %copy.32), calls=%async_computation.1 | async-start | bytes 3145728 | tf_op jit(solution)/shard_map/all_to_all | solution.py:36
  64.8 39.3 %reduce-scatter.5.cloned.1.call-start = ((), (), s32[]{:S(2)}) async-start(), calls=%async_computation.5 | async-start | bytes 655360 | tf_op jit(solution)/shard_map/reduce_scatter | solution.py:41
  69.7 55.3 %reduce-scatter.3.cloned.1.call-start = ((), (), s32[]{:S(2)}) async-start(), calls=%async_computation.4 | async-start | bytes 655360 | tf_op jit(solution)/shard_map/reduce_scatter | solution.py:40
  101.2 1.4 %copy-start.3 = (bf16[1536,512]{1,0:T(8,128)(2,1)S(1)}, bf16[1536,512]{1,0:T(8,128)(2,1)}, u32[]{:S(2)}) copy-start(bf16[1536,512]{1,0:T(8,128)(2,1)} %param.4) | copy-start | bytes 4718596
Sparse Core Ops, SparseCore 0:
  69.8 23.0 reduce-scatter.4
  104.1 20.7 reduce-scatter.2
where the time goes:
time: 134 us; the launch traced here: 133 us
  waiting for transfers between devices  83.2 us (62%)
  between operations  14.1 us (11%)
  local copies, waits for them, and re-layouts  14 us (10%)
  starting transfers between devices  10.1 us (8%)
  matrix products  8.54 us (6%)
  other arithmetic  3.34 us (2%)
    all_to_all x1, waiting for transfers between devices, on_device(): lax.all_to_all(outgoing, 'blk', split_axis=1, concat_axis=0, tiled=True)  32.4 us
    all_to_all x1, waiting for transfers between devices, on_device(): lax.all_to_all(backward_in, 'blk', split_axis=0, concat_axis=1, tiled=True)  31.5 us
    reduce_scatter x1, waiting for transfers between devices, on_device(): lax.psum_scatter(term_left, 'tok', scatter_dimension=1, tiled=True)  19.3 us
    unnamed x14, local copies, waits for them, and re-layouts  7.16 us
    all_to_all x1, starting transfers between devices, on_device(): lax.all_to_all(outgoing, 'blk', split_axis=1, concat_axis=0, tiled=True)  6.45 us
    all_to_all x1, starting transfers between devices, on_device(): lax.all_to_all(backward_in, 'blk', split_axis=0, concat_axis=1, tiled=True)  3.56 us
    mul x2, other arithmetic, on_device(): return (summed_left * inverse_rows, summed_right * inverse_rows)  3.14 us
    dot_general x1, matrix products, on_device(): jnp.einsum('got,kgmt->gokm', error_rows, mixed_part, preferred_element_ty...  2.79 us
  transfers between devices with their start and end apart: 4, of which 3 were waited for; matrix products, arithmetic and copies ran while one was open for 9% of the time, Pallas kernels for 0%

commit v1 on v0

--- a/solution.py
+++ b/solution.py
@@ -2,6 +2,22 @@
 import jax.numpy as jnp
 from jax import lax
 from jax.sharding import PartitionSpec as P
+
+
+def exchange_in_pairs(x, axis, split, join):
+    ways, here = (lax.axis_size(axis), lax.axis_index(axis))
+    width = x.shape[split] // ways
+    lengths = list(x.shape)
+    lengths[split] = width
+    height = lengths[join]
+    lengths[join] = height * ways
+    full = jnp.zeros(lengths, x.dtype)
+    for mask in range(ways):
+        part = lax.dynamic_slice_in_dim(x, (here ^ mask) * width, width, axis=split)
+        if mask:
+            part = lax.ppermute(part, axis, [(d, d ^ mask) for d in range(ways)])
+        full = lax.dynamic_update_slice_in_dim(full, part, (here ^ mask) * height, axis=join)
+    return full
 
 
 def on_device(inputs, targets, left_factor, right_factor):
@@ -17,7 +33,7 @@
     ).astype(jnp.bfloat16)
     outgoing = first_out.reshape(local_blocks, peer_count, local_blocks, stride_len, tok_rows)
     right_view = right_factor.reshape(local_blocks, block_width, all_blocks, stride_len)
-    arrived = lax.all_to_all(outgoing, "blk", split_axis=1, concat_axis=0, tiled=True)
+    arrived = exchange_in_pairs(outgoing, "blk", 1, 0)
     mixed_part = arrived[:, 0]
     student_part = jnp.einsum(
         "gokm,kgmt->got", right_view, mixed_part, preferred_element_type=jnp.float32

time: 134 us -> 128 us (0.955)
  waiting for transfers between devices: 83.2 us -> 72.2 us
  starting transfers between devices: 10.1 us -> 14.5 us
  local copies, waits for them, and re-layouts: 14 us -> 16.1 us
    all_to_all x1 -> x0, waiting for transfers between devices: 32.4 us -> none  [on_device(): lax.all_to_all(outgoing, 'blk', split_axis=1, concat_axis=0, tiled=True)]
    ppermute x0 -> x3, waiting for transfers between devices: none -> 21.9 us  [exchange_in_pairs(): part = lax.ppermute(part, axis, [(d, d ^ mask) for d in range(ways)])]
    all_to_all x1 -> x0, starting transfers between devices: 6.45 us -> none  [on_device(): lax.all_to_all(outgoing, 'blk', split_axis=1, concat_axis=0, tiled=True)]
    ppermute x0 -> x3, starting transfers between devices: none -> 5.62 us  [exchange_in_pairs(): part = lax.ppermute(part, axis, [(d, d ^ mask) for d in range(ways)])]
    all_to_all x1, starting transfers between devices: 3.56 us -> 8.8 us  [on_device(): lax.all_to_all(backward_in, 'blk', split_axis=0, concat_axis=1, tiled=True)]
    dynamic_update_slice x0 -> x4, local copies, waits for them, and re-layouts: none -> 3.1 us  [exchange_in_pairs(): lax.dynamic_update_slice_in_dim(full, part, (here ^ mask) * height, axis=...]
    unnamed x14 -> x19, local copies, waits for them, and re-layouts: 7.16 us -> 6.46 us
  transfers between devices with their start and end apart: 4 -> 6, of which waited for: 3 -> 4; matrix products, arithmetic and copies ran while one was open for 9% -> 11% of each run, Pallas kernels for 0% -> 0%
where the time goes in v1:
time: 128 us
  waiting for transfers between devices  72.2 us (56%)
  local copies, waits for them, and re-layouts  16.1 us (13%)
  starting transfers between devices  14.5 us (11%)
  between operations  14.2 us (11%)
  matrix products  7.53 us (6%)
  other arithmetic  3.34 us (3%)
    all_to_all x1, waiting for transfers between devices, on_device(): lax.all_to_all(backward_in, 'blk', split_axis=0, concat_axis=1, tiled=True)  30.9 us
    ppermute x3, waiting for transfers between devices, exchange_in_pairs(): part = lax.ppermute(part, axis, [(d, d ^ mask) for d in range(ways)])  21.9 us
    reduce_scatter x1, waiting for transfers between devices, on_device(): lax.psum_scatter(term_left, 'tok', scatter_dimension=1, tiled=True)  19.3 us
    all_to_all x1, starting transfers between devices, on_device(): lax.all_to_all(backward_in, 'blk', split_axis=0, concat_axis=1, tiled=True)  8.8 us
    unnamed x19, local copies, waits for them, and re-layouts  6.46 us
    ppermute x3, starting transfers between devices, exchange_in_pairs(): part = lax.ppermute(part, axis, [(d, d ^ mask) for d in range(ways)])  5.62 us
    mul x2, other arithmetic, on_device(): return (summed_left * inverse_rows, summed_right * inverse_rows)  3.14 us
    dynamic_update_slice x4, local copies, waits for them, and re-layouts, exchange_in_pairs(): lax.dynamic_update_slice_in_dim(full, part, (here ^ mask) * height, axis=...  3.1 us
  transfers between devices with their start and end apart: 6, of which 4 were waited for; matrix products, arithmetic and copies ran while one was open for 11% of the time, Pallas kernels for 0%

profile of v1, /device:TPU:0, one launch (start us, length us, event | category | flops | bytes accessed | tf_op | source)
XLA Modules:
  0.0 127.8 jit_solution(15357030064259505837)
XLA Ops:
  7.2 0.9 copy-done
  8.1 2.0 %convolution_convert_fusion = bf16[2,256,1536]{2,1,0:T(8,128)(2,1)S(1)} fusion(bf16[2,256,256]{2,1,0:T(8,128)(2,1)S(1)} %copy-done, bf16[192,2,8,256]{3,2,1,0:T(8,128)(2,1)} %bitcast.58), kind=kOutput, calls=%fused_computation.3 | convolution fusion | flops 403439616 | bytes 3407872 | tf_op jit(solution)/shard_map/tki,kji->kjt/dot_general | solution.py:31
  10.1 0.9 constant_dynamic-slice_fusion
  11.0 0.8 copy.50
  11.8 3.0 %collective-permute-start = (bf16[2,1,2,32,1536]{4,3,0,2,1:T(8,128)(2,1)}, bf16[2,1,2,32,1536]{4,3,0,2,1:T(8,128)(2,1)}, u32[]{:S(2)}, u32[]{:S(2)}) collective-permute-start(bf16[2,1,2,32,1536]{4,3,0,2,1:T(8,128)(2,1)} %copy.50), channel_id=1, source_target_pairs={{0,4},{4,0},{8,12},{12,8},{1,5},{5,1},{9,13},{13,9},{2,6},{6,2},{1... | collective-permute-start | bytes 1179656 | tf_op jit(solution)/shard_map/ppermute | solution.py:18
  14.8 0.8 copy.51
  15.6 2.6 %collective-permute-start.1 = (bf16[2,1,2,32,1536]{4,3,0,2,1:T(8,128)(2,1)}, bf16[2,1,2,32,1536]{4,3,0,2,1:T(8,128)(2,1)}, u32[]{:S(2)}, u32[]{:S(2)}) collective-permute-start(bf16[2,1,2,32,1536]{4,3,0,2,1:T(8,128)(2,1)} %copy.51), channel_id=1, source_target_pairs={{0,8},{4,12},{8,0},{12,4},{1,9},{5,13},{9,1},{13,5},{2,10},{6,14},... | collective-permute-start | bytes 1179656 | tf_op jit(solution)/shard_map/ppermute | solution.py:18
  18.2 0.8 copy.52
  19.7 2.0 %copy.38 = f32[1536,2,256]{2,0,1:T(8,128)} copy(bf16[1536,2,256]{0,2,1:T(8,128)(2,1)S(1)} %bitcast.55) | data formatting | bytes 4718592 | tf_op jit(solution)/shard_map/convert_element_type | solution.py:44
  22.8 8.8 %collective-permute-done = bf16[2,1,2,32,1536]{4,3,0,2,1:T(8,128)(2,1)} collective-permute-done((bf16[2,1,2,32,1536]{4,3,0,2,1:T(8,128)(2,1)}, bf16[2,1,2,32,1536]{4,3,0,2,1:T(8,128)(2,1)}, u32[]{:S(2)}, u32[]{:S(2)}) %collective-permute-start) | collective-permute-done | bytes 393248 | tf_op jit(solution)/shard_map/ppermute | solution.py:18
  31.5 1.0 bitcast_dynamic-update-slice_fusion.2
  32.6 13.1 %collective-permute-done.1 = bf16[2,1,2,32,1536]{4,3,0,2,1:T(8,128)(2,1)} collective-permute-done((bf16[2,1,2,32,1536]{4,3,0,2,1:T(8,128)(2,1)}, bf16[2,1,2,32,1536]{4,3,0,2,1:T(8,128)(2,1)}, u32[]{:S(2)}, u32[]{:S(2)}) %collective-permute-start.1) | collective-permute-done | bytes 393248 | tf_op jit(solution)/shard_map/ppermute | solution.py:18
  45.7 1.0 bitcast_dynamic-update-slice_fusion.1
  46.7 1.0 bitcast_dynamic-update-slice_fusion
  49.8 1.3 %copy.40 = bf16[8,2,32,1536]{3,2,1,0:T(8,128)(2,1)} copy(bf16[8,2,32,1536]{3,2,0,1:T(8,128)(2,1)S(1)} %convert_bitcast_fusion) | data formatting | bytes 3145728 | tf_op jit(solution)/shard_map/convert_element_type | solution.py:51
  51.1 8.8 %all-to-all-start = ((bf16[8,2,32,1536]{3,2,1,0:T(8,128)(2,1)}), bf16[8,2,32,1536]{3,2,1,0:T(8,128)(2,1)S(1)}, u32[]{:S(2)}, u32[]{:S(2)}) async-start(bf16[8,2,32,1536]{3,2,1,0:T(8,128)(2,1)} %copy.40), calls=%async_computation | async-start | bytes 3145728 | tf_op jit(solution)/shard_map/all_to_all | solution.py:52
  59.9 2.8 %fusion.5 = f32[2,256,8,32]{1,3,2,0:T(8,128)} fusion(bf16[8,2,32,1536]{3,2,0,1:T(8,128)(2,1)} %copy-done.3, bf16[2,256,1536]{1,2,0:T(8,128)(2,1)S(1)} %fusion.1), kind=kOutput, calls=%fused_computation.7 | convolution fusion | flops 402653184 | bytes 3670016 | tf_op jit(solution)/shard_map/got,kgmt->gokm/dot_general | solution.py:46
  62.6 2.0 %copy.44 = f32[2,256,256]{2,1,0:T(8,128)} copy(f32[2,256,256]{1,2,0:T(8,128)} %bitcast.60) | data formatting | bytes 1048576 | tf_op jit(solution)/shard_map/reshape | solution.py:48
  64.8 30.9 %all-to-all-done = bf16[8,2,32,1536]{3,2,1,0:T(8,128)(2,1)S(1)} async-done(((bf16[8,2,32,1536]{3,2,1,0:T(8,128)(2,1)}), bf16[8,2,32,1536]{3,2,1,0:T(8,128)(2,1)S(1)}, u32[]{:S(2)}, u32[]{:S(2)}) %all-to-all-start) | async-done | bytes 1572896 | tf_op jit(solution)/shard_map/all_to_all | solution.py:52
  95.8 1.3 %copy-done.4 = bf16[1536,512]{1,0:T(8,128)(2,1)S(1)} copy-done((bf16[1536,512]{1,0:T(8,128)(2,1)S(1)}, bf16[1536,512]{1,0:T(8,128)(2,1)}, u32[]{:S(2)}) %copy-start.4) | copy-done | bytes 1572888
  97.1 1.4 %fusion.2 = f32[2,256,256]{2,1,0:T(8,128)} fusion(bf16[2,256,1536]{2,1,0:T(8,128)(2,1)S(1)} %bitcast.57, bf16[192,2,8,256]{3,2,1,0:T(8,128)(2,1)S(1)} %bitcast.59), kind=kOutput, calls=%fused_computation.4 | convolution fusion | flops 402653184 | bytes 3670016 | tf_op jit(solution)/shard_map/kjt,tki->kji/dot_general | solution.py:54
  98.5 1.6 %broadcast_multiply_fusion = f32[2,64,256]{2,1,0:T(8,128)} fusion(f32[2,64,256]{2,1,0:T(8,128)} %reduce-scatter.5.cloned.1.call-done), kind=kLoop, calls=%fused_computation.16 | loop fusion | flops 32768 | bytes 262144 | tf_op jit(solution)/shard_map/mul | solution.py:59
  100.1 19.3 %reduce-scatter.3.cloned.1.call-done = f32[2,64,256]{2,1,0:T(8,128)} async-done(((f32[2,256,256]{2,1,0:T(8,128)}), f32[2,64,256]{2,1,0:T(8,128)}) %reduce-scatter.3.cloned.1.call-update) | async-done | bytes 131088 | tf_op jit(solution)/shard_map/reduce_scatter | solution.py:56
  119.4 1.6 %broadcast_multiply_fusion.1 = f32[2,64,256]{2,1,0:T(8,128)} fusion(f32[2,64,256]{2,1,0:T(8,128)} %reduce-scatter.3.cloned.1.call-done), kind=kLoop, calls=%fused_computation.17 | loop fusion | flops 32768 | bytes 262144 | tf_op jit(solution)/shard_map/mul | solution.py:59
  (27 shorter events, 3.9 us)
Async XLA Ops:
  7.2 1.0 copy-start
  11.0 8.0 %copy-start.2 = (bf16[1536,512]{1,0:T(8,128)(2,1)S(1)}, bf16[1536,512]{1,0:T(8,128)(2,1)}, u32[]{:S(2)}) copy-start(bf16[1536,512]{1,0:T(8,128)(2,1)} %param.5) | copy-start | bytes 4718596
  11.8 19.7 %collective-permute-start = (bf16[2,1,2,32,1536]{4,3,0,2,1:T(8,128)(2,1)}, bf16[2,1,2,32,1536]{4,3,0,2,1:T(8,128)(2,1)}, u32[]{:S(2)}, u32[]{:S(2)}) collective-permute-start(bf16[2,1,2,32,1536]{4,3,0,2,1:T(8,128)(2,1)} %copy.50), channel_id=1, source_target_pairs={{0,4},{4,0},{8,12},{12,8},{1,5},{5,1},{9,13},{13,9},{2,6},{6,2},{1... | collective-permute-start | bytes 1179656 | tf_op jit(solution)/shard_map/ppermute | solution.py:18
  15.6 30.1 %collective-permute-start.1 = (bf16[2,1,2,32,1536]{4,3,0,2,1:T(8,128)(2,1)}, bf16[2,1,2,32,1536]{4,3,0,2,1:T(8,128)(2,1)}, u32[]{:S(2)}, u32[]{:S(2)}) collective-permute-start(bf16[2,1,2,32,1536]{4,3,0,2,1:T(8,128)(2,1)} %copy.51), channel_id=1, source_target_pairs={{0,8},{4,12},{8,0},{12,4},{1,9},{5,13},{9,1},{13,5},{2,10},{6,14},... | collective-permute-start | bytes 1179656 | tf_op jit(solution)/shard_map/ppermute | solution.py:18
  19.0 27.8 %collective-permute-start.2 = (bf16[2,1,2,32,1536]{4,3,0,2,1:T(8,128)(2,1)}, bf16[2,1,2,32,1536]{4,3,0,2,1:T(8,128)(2,1)}, u32[]{:S(2)}, u32[]{:S(2)}) collective-permute-start(bf16[2,1,2,32,1536]{4,3,0,2,1:T(8,128)(2,1)} %copy.52), channel_id=1, source_target_pairs={{0,12},{4,8},{8,4},{12,0},{1,13},{5,9},{9,5},{13,1},{2,14},{6,10},... | collective-permute-start | bytes 1179656 | tf_op jit(solution)/shard_map/ppermute | solution.py:18
  19.7 2.1 %copy-start.6 = (bf16[2,256,256]{2,1,0:T(8,128)(2,1)S(1)}, bf16[2,256,256]{2,1,0:T(8,128)(2,1)}, u32[]{:S(2)}) copy-start(bf16[2,256,256]{2,1,0:T(8,128)(2,1)} %param.7) | copy-start | bytes 786436
  21.7 1.0 copy-start.5
  22.7 25.1 %copy-start.1 = (f32[1536,2,256]{2,0,1:T(8,128)S(1)}, f32[1536,2,256]{2,0,1:T(8,128)}, u32[]{:S(2)}) copy-start(f32[1536,2,256]{2,0,1:T(8,128)} %copy.38) | copy-start | bytes 9437188
  47.8 1.2 copy-start.3
  51.1 44.6 %all-to-all-start = ((bf16[8,2,32,1536]{3,2,1,0:T(8,128)(2,1)}), bf16[8,2,32,1536]{3,2,1,0:T(8,128)(2,1)S(1)}, u32[]{:S(2)}, u32[]{:S(2)}) async-start(bf16[8,2,32,1536]{3,2,1,0:T(8,128)(2,1)} %copy.40), calls=%async_computation | async-start | bytes 3145728 | tf_op jit(solution)/shard_map/all_to_all | solution.py:52
  59.9 38.6 %reduce-scatter.5.cloned.1.call-start = ((), (), s32[]{:S(2)}) async-start(), calls=%async_computation.4 | async-start | bytes 655360 | tf_op jit(solution)/shard_map/reduce_scatter | solution.py:57
  64.7 54.7 %reduce-scatter.3.cloned.1.call-start = ((), (), s32[]{:S(2)}) async-start(), calls=%async_computation.3 | async-start | bytes 655360 | tf_op jit(solution)/shard_map/reduce_scatter | solution.py:56
  95.7 1.4 %copy-start.4 = (bf16[1536,512]{1,0:T(8,128)(2,1)S(1)}, bf16[1536,512]{1,0:T(8,128)(2,1)}, u32[]{:S(2)}) copy-start(bf16[1536,512]{1,0:T(8,128)(2,1)} %param.4) | copy-start | bytes 4718596
Sparse Core Ops, SparseCore 0:
  64.8 23.1 reduce-scatter.4
  98.6 20.7 reduce-scatter.2
